TPU v7x, 32 devices: a whole 2x2x4 slice. The times are simulated.
32 devices in a mesh: row: 4 (over z), col: 8 (over y, x, core).
Axes of the slice: x: 2, y: 2, z: 4, core: 2. Of those that a mesh axis runs over, the one named last changes fastest.
Arguments:
- pair: bfloat16 [128, 128, 128], P('row', 'col'), may hold values from -6 to 6
- gain_in: float32 [128], replicated, may hold values from 0.1 to 1.9
- w_left_gate: bfloat16 [128, 128], replicated, may hold values from -0.5 to 0.5
- w_left: bfloat16 [128, 128], replicated, may hold values from -0.5 to 0.5
- w_right_gate: bfloat16 [128, 128], replicated, may hold values from -0.5 to 0.5
- w_right: bfloat16 [128, 128], replicated, may hold values from -0.5 to 0.5
- gain_out: float32 [128], replicated, may hold values from 0.1 to 1.9
- w_out_gate: bfloat16 [128, 128], replicated, may hold values from -0.5 to 0.5
- w_out: bfloat16 [128, 128], replicated, may hold values from -0.5 to 0.5
Outputs:
- update: bfloat16 [128, 128, 128], P('row', 'col')
All inputs are finite; a program needn't handle non-finite values.
Results may differ from a plain program's by a relative error of at most 0.0081.
Values may be sent and summed in bfloat16 or wider, within the bound.
A program may use at most 64 MiB of HBM per device.

v0:
```python
import jax
import jax.numpy as jnp
from jax import lax
from jax.sharding import PartitionSpec as P


def spread(value, axis, source):
    kept = jnp.where(lax.axis_index(axis) == source, value, 0).astype(value.dtype)
    return lax.psum(kept, axis)


def layer_norm(values, gain):
    mean = jnp.mean(values, axis=-1, keepdims=True)
    centred = values - mean
    variance = jnp.mean(centred * centred, axis=-1, keepdims=True)
    return centred * lax.rsqrt(variance + 1e-05) * gain


def project(normed, weight):
    return jnp.einsum("ijc,ch->ijh", normed, weight, preferred_element_type=jnp.float32)


def per_device(
    pair, gain_in, w_left_gate, w_left, w_right_gate, w_right, gain_out, w_out_gate, w_out
):
    col_block = pair.shape[1]
    normed = layer_norm(pair.astype(jnp.float32), gain_in).astype(jnp.bfloat16)
    left = (jax.nn.sigmoid(project(normed, w_left_gate)) * project(normed, w_left)).astype(
        jnp.bfloat16
    )
    right = (jax.nn.sigmoid(project(normed, w_right_gate)) * project(normed, w_right)).astype(
        jnp.bfloat16
    )
    panel = lax.all_gather(right, "col", axis=1, tiled=True)
    ratio = lax.axis_size("col") // lax.axis_size("row")
    column = lax.axis_index("col")
    owned = lax.dynamic_slice_in_dim(panel, column % ratio * col_block, col_block, 0)
    right_cols = spread(owned, "row", column // ratio)
    mixed = jnp.einsum(
        "ikh,jkh->ijh",
        lax.all_gather(left, "col", axis=1, tiled=True),
        right_cols,
        preferred_element_type=jnp.float32,
    )
    out_normed = layer_norm(mixed, gain_out).astype(jnp.bfloat16)
    gate = jax.nn.sigmoid(project(normed, w_out_gate))
    return (gate * project(out_normed, w_out)).astype(jnp.bfloat16)


def solution(mesh):
    return jax.shard_map(
        per_device,
        mesh=mesh,
        in_specs=(P("row", "col", None), P(), P(), P(), P(), P(), P(), P(), P()),
        out_specs=P("row", "col", None),
        check_vma=False,
    )
```

profile of v0, /device:TPU:0, one launch (start us, length us, event | category | flops | bytes accessed | tf_op | source)
XLA Modules:
  0.0 118.3 jit_solution(17860925446135129522)
XLA Ops:
  6.5 0.0 copy-start
  6.5 0.0 all-gather.3.cloned.1.call-start
  6.6 1.1 convert_reduce_fusion
  7.7 0.1 copy.27
  7.8 0.1 copy.28
  7.8 1.1 fusion.14
  9.0 0.1 copy.29
  9.1 0.1 copy.30
  9.2 0.0 copy-done
  9.2 1.2 %fusion.5 = f32[32,16,128]{2,1,0:T(8,128)S(1)} fusion(bf16[128,128]{1,0:T(8,128)(2,1)S(1)} %copy-done, bf16[32,16,128]{2,1,0:T(8,128)(2,1)} %param.9, f32[128]{0:T(128)} %param.10, f32[32,16]{1,0:T(8,128)S(1)} %copy.30, f32[32,16]{1,0:T(8,128)S(1)} %copy.28), kind=kOutput, calls=%fused_computation.11 | convolution fusion | flops 17301504 | bytes 430592 | tf_op jit(solution)/shard_map/ijc,ch->ijh/dot_general | solution.py:20
  10.4 1.9 %fusion.9 = bf16[32,16,128]{2,1,0:T(8,128)(2,1)} fusion(f32[32,16,128]{2,1,0:T(8,128)S(1)} %fusion.5, bf16[128,128]{1,0:T(8,128)(2,1)} %param.14, bf16[32,16,128]{2,1,0:T(8,128)(2,1)} %param.9, f32[128]{0:T(128)} %param.10, f32[32,16]{1,0:T(8,128)S(1)} %copy.30, f32[32,16]{1,0:T(8,128)S(1)} %copy.28), kind=kOutput, calls=%fused_computation.16 | convolution fusion | flops 17235968 | bytes 561664 | tf_op jit(solution)/shard_map/ijc,ch->ijh/dot_general | solution.py:20
  12.3 0.0 all-gather.3.cloned.1.call-update
  12.3 0.0 all-gather.5.cloned.1.call-start
  12.4 1.3 %fusion.2 = f32[32,16,128]{2,1,0:T(8,128)S(1)} fusion(bf16[128,128]{1,0:T(8,128)(2,1)} %param.11, bf16[32,16,128]{2,1,0:T(8,128)(2,1)} %param.9, f32[128]{0:T(128)} %param.10, f32[32,16]{1,0:T(8,128)S(1)} %copy.30, f32[32,16]{1,0:T(8,128)S(1)} %copy.28), kind=kOutput, calls=%fused_computation.7 | convolution fusion | flops 17301504 | bytes 430592 | tf_op jit(solution)/shard_map/ijc,ch->ijh/dot_general | solution.py:20
  13.7 1.9 %fusion.10 = bf16[32,16,128]{2,1,0:T(8,128)(2,1)} fusion(f32[32,16,128]{2,1,0:T(8,128)S(1)} %fusion.2, bf16[128,128]{1,0:T(8,128)(2,1)} %param.12, bf16[32,16,128]{2,1,0:T(8,128)(2,1)} %param.9, f32[128]{0:T(128)} %param.10, f32[32,16]{1,0:T(8,128)S(1)} %copy.30, f32[32,16]{1,0:T(8,128)S(1)} %copy.28), kind=kOutput, calls=%fused_computation.17 | convolution fusion | flops 17235968 | bytes 561664 | tf_op jit(solution)/shard_map/ijc,ch->ijh/dot_general | solution.py:20
  15.6 0.0 all-gather.5.cloned.1.call-update
  15.6 0.0 all-reduce.2.cloned.1.call-start
  15.7 23.1 %all-gather.3.cloned.1.call-done = bf16[32,128,128]{2,1,0:T(8,128)(2,1)} async-done(((bf16[32,16,128]{2,1,0:T(8,128)(2,1)}), bf16[32,128,128]{2,1,0:T(8,128)(2,1)}) %all-gather.3.cloned.1.call-update) | async-done | bytes 1048592 | tf_op jit(solution)/shard_map/all_gather | solution.py:34
  38.7 1.9 %dynamic-slice_select_fusion = bf16[16,128,128]{2,1,0:T(8,128)(2,1)} fusion(bf16[32,128,128]{2,1,0:T(8,128)(2,1)} %all-gather.3.cloned.1.call-done, s32[]{:T(128)S(6)} %select_n.25, pred[]{:T(512)S(6)} %eq.5), kind=kLoop, calls=%fused_computation.21 | loop fusion | flops 262144 | bytes 1048581 | tf_op jit(solution)/shard_map/jit(_where)/select_n | solution.py:8
  40.6 0.0 all-reduce.2.cloned.1.call-update
  40.6 0.0 copy-done.1
  40.6 0.3 fusion.8
  41.0 23.1 %all-gather.5.cloned.1.call-done = bf16[32,128,128]{2,1,0:T(8,128)(2,1)} async-done(((bf16[32,16,128]{2,1,0:T(8,128)(2,1)}), bf16[32,128,128]{2,1,0:T(8,128)(2,1)}) %all-gather.5.cloned.1.call-update) | async-done | bytes 1048592 | tf_op jit(solution)/shard_map/all_gather | solution.py:41
  64.1 8.6 %copy.32 = bf16[32,128,128]{0,1,2:T(8,128)(2,1)} copy(bf16[32,128,128]{2,1,0:T(8,128)(2,1)} %all-gather.5.cloned.1.call-done) | data formatting | bytes 2097152 | tf_op jit(solution)/shard_map/all_gather | solution.py:41
  72.7 32.4 %all-reduce.2.cloned.1.call-done = bf16[16,128,128]{2,1,0:T(8,128)(2,1)} async-done(((bf16[16,128,128]{2,1,0:T(8,128)(2,1)}), bf16[16,128,128]{2,1,0:T(8,128)(2,1)}) %all-reduce.2.cloned.1.call-update) | async-done | bytes 524304 | tf_op jit(solution)/shard_map/psum | solution.py:9
  105.1 1.5 %copy.31 = bf16[16,128,128]{1,0,2:T(8,128)(2,1)S(1)} copy(bf16[16,128,128]{2,1,0:T(8,128)(2,1)} %all-reduce.2.cloned.1.call-done) | data formatting | bytes 1048576 | tf_op jit(solution)/shard_map/psum | solution.py:9
  106.6 0.0 copy-start.2
  106.6 3.4 %fusion.28 = (f32[32,16]{0,1:T(8,128)S(1)}, f32[32,16,128]{0,1,2:T(8,128)S(1)}) fusion(bf16[16,128,128]{1,0,2:T(8,128)(2,1)S(1)} %copy.31, bf16[32,128,128]{0,1,2:T(8,128)(2,1)} %copy.32), kind=kOutput, calls=%fused_computation.39 | convolution fusion | flops 16842240 | bytes 1837056 | tf_op jit(solution)/shard_map/ikh,jkh->ijh/dot_general | solution.py:39
  110.0 0.2 multiply_reduce_fusion
  110.2 0.2 multiply_convert_fusion
  110.4 0.5 copy.33
  110.9 0.8 fusion.11
  (12 shorter events, 0.0 us)
Async XLA Ops:
  6.5 2.6 %copy-start = (bf16[128,128]{1,0:T(8,128)(2,1)S(1)}, bf16[128,128]{1,0:T(8,128)(2,1)}, u32[]{:S(2)}) copy-start(bf16[128,128]{1,0:T(8,128)(2,1)} %param.13) | copy-start | bytes 98308
  6.5 34.1 %copy-start.1 = (bf16[32,16,128]{2,1,0:T(8,128)(2,1)S(1)}, bf16[32,16,128]{2,1,0:T(8,128)(2,1)}, u32[]{:S(2)}) copy-start(bf16[32,16,128]{2,1,0:T(8,128)(2,1)} %param.9) | copy-start | bytes 393220
  6.5 34.1 %copy-start.3 = (f32[128]{0:T(128)S(1)}, f32[128]{0:T(128)}, u32[]{:S(2)}) copy-start(f32[128]{0:T(128)} %param.10) | copy-start | bytes 1540
  6.5 34.1 %copy-start.5 = (bf16[128,128]{1,0:T(8,128)(2,1)S(1)}, bf16[128,128]{1,0:T(8,128)(2,1)}, u32[]{:S(2)}) copy-start(bf16[128,128]{1,0:T(8,128)(2,1)} %param.16) | copy-start | bytes 98308
  6.5 32.2 %all-gather.3.cloned.1.call-start = ((), (), s32[]{:S(2)}) async-start(), calls=%async_computation | async-start | bytes 1179648 | tf_op jit(solution)/shard_map/all_gather | solution.py:34
  12.3 51.7 %all-gather.5.cloned.1.call-start = ((), (), s32[]{:S(2)}) async-start(), calls=%async_computation.2 | async-start | bytes 1179648 | tf_op jit(solution)/shard_map/all_gather | solution.py:41
  15.6 89.5 %all-reduce.2.cloned.1.call-start = ((), (), s32[]{:S(2)}) async-start(), calls=%async_computation.1 | async-start | bytes 1048576 | tf_op jit(solution)/shard_map/psum | solution.py:9
  72.7 37.5 %copy-start.4 = (f32[128]{0:T(128)S(1)}, f32[128]{0:T(128)}, u32[]{:S(2)}) copy-start(f32[128]{0:T(128)} %param.15) | copy-start | bytes 1540
  106.6 4.4 %copy-start.2 = (bf16[128,128]{1,0:T(8,128)(2,1)S(1)}, bf16[128,128]{1,0:T(8,128)(2,1)}, u32[]{:S(2)}) copy-start(bf16[128,128]{1,0:T(8,128)(2,1)} %param.17) | copy-start | bytes 98308
Sparse Core Ops, SparseCore 0:
  12.5 26.1 all-gather.2
  40.6 23.4 all-gather.4
  66.4 38.6 all-reduce.1
where the time goes:
time: 119 us; the launch traced here: 118 us
  waiting for transfers between devices  78.6 us (66%)
  between operations  13.3 us (11%)
  local copies, waits for them, and re-layouts  10.9 us (9%)
  matrix products  10.9 us (9%)
  other arithmetic  4.59 us (4%)
    psum x1, waiting for transfers between devices, spread(): return lax.psum(kept, axis)  32.4 us
    all_gather x1, waiting for transfers between devices, per_device(): lax.all_gather(left, 'col', axis=1, tiled=True)  23.1 us
    all_gather x1, waiting for transfers between devices, per_device(): panel = lax.all_gather(right, 'col', axis=1, tiled=True)  23.1 us
    all_gather x1, local copies, waits for them, and re-layouts, per_device(): lax.all_gather(left, 'col', axis=1, tiled=True)  8.61 us
    dot_general x6, matrix products, project(): jnp.einsum('ijc,ch->ijh', normed, weight, preferred_element_type=jnp.floa...  7.46 us
    dot_general x1, matrix products, per_device(): jnp.einsum('ikh,jkh->ijh', lax.all_gather(left, 'col', axis=1, tiled=True...  3.39 us
  transfers between devices with their start and end apart: 3, of which 3 were waited for; matrix products, arithmetic and copies ran while one was open for 12% of the time, Pallas kernels for 0%

commit v1 on v0

--- a/solution.py
+++ b/solution.py
@@ -2,6 +2,12 @@
 import jax.numpy as jnp
 from jax import lax
 from jax.sharding import PartitionSpec as P
+
+
+def work_the_pages(view, row_dim):
+    y_new = list(view.shape[1:])
+    y_new[row_dim] *= view.shape[0]
+    return jnp.moveaxis(view, 0, row_dim).reshape(y_new)
 
 
 def spread(value, axis, source):
@@ -36,11 +42,32 @@
     column = lax.axis_index("col")
     owned = lax.dynamic_slice_in_dim(panel, column % ratio * col_block, col_block, 0)
     right_cols = spread(owned, "row", column // ratio)
+
+    def _lead_ends(in_array, chip_axis, axis_k):
+        chips = lax.axis_size(chip_axis)
+        all_rows = [(dev, (dev + 1) % chips) for dev in range(chips)]
+        buffer = [(idx, num) for num, idx in all_rows]
+        last, near = ([], [])
+        for s in tuple(range(chips - 1)):
+            if s % 2 == 0:
+                tile_out = lax.ppermute(
+                    last[-1] if last else in_array, axis_name=chip_axis, perm=all_rows
+                )
+                last.append(tile_out)
+            else:
+                upper = lax.ppermute(
+                    near[-1] if near else in_array, axis_name=chip_axis, perm=buffer
+                )
+                near.append(upper)
+        o_now = jnp.stack([*last[::-1], in_array, *near])
+        local_out = lax.axis_index(chip_axis)
+        y = len(last)
+        u_next = local_out - y
+        o_now = o_now[(jnp.arange(chips) - u_next) % chips]
+        return work_the_pages(o_now, axis_k)
+
     mixed = jnp.einsum(
-        "ikh,jkh->ijh",
-        lax.all_gather(left, "col", axis=1, tiled=True),
-        right_cols,
-        preferred_element_type=jnp.float32,
+        "ikh,jkh->ijh", _lead_ends(left, "col", 1), right_cols, preferred_element_type=jnp.float32
     )
     out_normed = layer_norm(mixed, gain_out).astype(jnp.bfloat16)
     gate = jax.nn.sigmoid(project(normed, w_out_gate))

time: 119 us -> 93 us (0.78)
  waiting for transfers between devices: 78.6 us -> 55.7 us
  starting transfers between devices: 0.12 us -> 8.57 us
  matrix products: 10.9 us -> 4.47 us
  local copies, waits for them, and re-layouts: 10.9 us -> 6.5 us
    all_gather x1 -> x0, waiting for transfers between devices: 23.1 us -> none  [per_device(): lax.all_gather(left, 'col', axis=1, tiled=True)]
    all_gather x1, waiting for transfers between devices: 23.1 us -> 4.05 us  [per_device(): panel = lax.all_gather(right, 'col', axis=1, tiled=True)]
    ppermute x0 -> x7, waiting for transfers between devices: none -> 14 us  [the longest x4 14 us: _lead_ends(): lax.ppermute(last[-1] if last else in_array, axis_name=chip_axis, perm=al...]
    all_gather x1 -> x0, local copies, waits for them, and re-layouts: 8.61 us -> none  [per_device(): lax.all_gather(left, 'col', axis=1, tiled=True)]
    ppermute x0 -> x7, starting transfers between devices: none -> 8.53 us  [the longest x3 7.98 us: _lead_ends(): lax.ppermute(near[-1] if near else in_array, axis_name=chip_axis, perm=bu...]
    psum x1, waiting for transfers between devices: 32.4 us -> 37.6 us  [spread(): return lax.psum(kept, axis)]
    dot_general x6, matrix products: 7.46 us -> 3.81 us  [project(): jnp.einsum('ijc,ch->ijh', normed, weight, preferred_element_type=jnp.floa...]
    dot_general x1, matrix products: 3.39 us -> 0.66 us  [per_device(): jnp.einsum('ikh,jkh->ijh', _lead_ends(left, 'col', 1), right_cols, prefer...]
  transfers between devices with their start and end apart: 3 -> 9, of which waited for: 3 -> 6; matrix products, arithmetic and copies ran while one was open for 12% -> 7% of each run, Pallas kernels for 0% -> 0%
where the time goes in v1:
time: 93 us; the launch traced here: 92.6 us
  waiting for transfers between devices  55.7 us (60%)
  between operations  13.7 us (15%)
  starting transfers between devices  8.57 us (9%)
  local copies, waits for them, and re-layouts  6.5 us (7%)
  matrix products  4.47 us (5%)
  other arithmetic  3.71 us (4%)
    psum x1, waiting for transfers between devices, spread(): return lax.psum(kept, axis)  37.6 us
    ppermute x4, waiting for transfers between devices, _lead_ends(): lax.ppermute(last[-1] if last else in_array, axis_name=chip_axis, perm=al...  14 us
    ppermute x3, starting transfers between devices, _lead_ends(): lax.ppermute(near[-1] if near else in_array, axis_name=chip_axis, perm=bu...  7.98 us
    all_gather x1, waiting for transfers between devices, per_device(): panel = lax.all_gather(right, 'col', axis=1, tiled=True)  4.05 us
    dot_general x6, matrix products, project(): jnp.einsum('ijc,ch->ijh', normed, weight, preferred_element_type=jnp.floa...  3.81 us
    unnamed x27, local copies, waits for them, and re-layouts  2.22 us
    select_n x1, other arithmetic, spread(): jnp.where(lax.axis_index(axis) == source, value, 0).astype(value.dtype)  1.9 us
  transfers between devices with their start and end apart: 9, of which 6 were waited for; matrix products, arithmetic and copies ran while one was open for 7% of the time, Pallas kernels for 0%

profile of v1, /device:TPU:0, one launch (start us, length us, event | category | flops | bytes accessed | tf_op | source)
XLA Modules:
  0.0 92.6 jit_solution(1647002349421057554)
XLA Ops:
  6.5 1.1 %convert_reduce_fusion = f32[32,16]{1,0:T(8,128)S(1)} fusion(bf16[32,16,128]{2,1,0:T(8,128)(2,1)} %param.9), kind=kLoop, calls=%fused_computation.24 | loop fusion | flops 130560 | bytes 133120 | tf_op jit(solution)/shard_map/reduce_sum | solution.py:19
  7.7 0.1 copy.35
  7.8 0.2 fusion.14
  8.2 0.6 copy-done.6
  8.8 0.3 fusion.2
  9.2 0.4 copy-done.4
  9.6 0.3 fusion.10
  9.9 0.5 collective-permute-start
  10.4 0.3 fusion.5
  10.8 1.0 %fusion.9 = bf16[32,16,128]{2,1,0:T(8,128)(2,1)} fusion(f32[32,16,128]{2,1,0:T(8,128)S(1)} %fusion.5, bf16[128,128]{1,0:T(8,128)(2,1)S(1)} %copy-done.5, bf16[32,16,128]{2,1,0:T(8,128)(2,1)S(1)} %copy-done.1, f32[128]{0:T(128)S(1)} %copy-done.6, f32[32,16]{1,0:T(8,128)S(1)} %copy.37, f32[32,16]{1,0:T(8,128)S(1)} %copy.35), kind=kOutput, calls=%fused_computation.17 | convolution fusion | flops 17235968 | bytes 561664 | tf_op jit(solution)/shard_map/ijc,ch->ijh/dot_general | solution.py:26
  11.9 4.1 %collective-permute-done = bf16[32,16,128]{2,1,0:T(8,128)(2,1)S(1)} collective-permute-done((bf16[32,16,128]{2,1,0:T(8,128)(2,1)S(1)}, bf16[32,16,128]{2,1,0:T(8,128)(2,1)S(1)}, u32[]{:S(2)}, u32[]{:S(2)}) %collective-permute-start) | collective-permute-done | bytes 131104 | tf_op jit(solution)/shard_map/ppermute | solution.py:53
  16.0 2.6 %collective-permute-start.4 = (bf16[32,16,128]{2,1,0:T(8,128)(2,1)S(1)}, bf16[32,16,128]{2,1,0:T(8,128)(2,1)S(1)}, u32[]{:S(2)}, u32[]{:S(2)}) collective-permute-start(bf16[32,16,128]{2,1,0:T(8,128)(2,1)S(1)} %fusion.10), channel_id=1, source_target_pairs={{1,0},{2,1},{3,2},{4,3},{5,4},{6,5},{7,6},{0,7},{9,8},{10,9},{11,1... | collective-permute-start | bytes 393224 | tf_op jit(solution)/shard_map/ppermute | solution.py:58
  18.6 2.6 %collective-permute-done.1 = bf16[32,16,128]{2,1,0:T(8,128)(2,1)S(1)} collective-permute-done((bf16[32,16,128]{2,1,0:T(8,128)(2,1)S(1)}, bf16[32,16,128]{2,1,0:T(8,128)(2,1)S(1)}, u32[]{:S(2)}, u32[]{:S(2)}) %collective-permute-start.1) | collective-permute-done | bytes 131104 | tf_op jit(solution)/shard_map/ppermute | solution.py:53
  21.3 1.0 %fusion.8 = f32[32,16,128]{2,1,0:T(8,128)} fusion(bf16[128,128]{1,0:T(8,128)(2,1)S(1)} %copy-done.9, bf16[32,16,128]{2,1,0:T(8,128)(2,1)S(1)} %copy-done.1, f32[128]{0:T(128)S(1)} %copy-done.6, f32[32,16]{1,0:T(8,128)S(1)} %copy.37, f32[32,16]{1,0:T(8,128)S(1)} %copy.35), kind=kOutput, calls=%fused_computation.16 | convolution fusion | flops 17301504 | bytes 430592 | tf_op jit(solution)/shard_map/ijc,ch->ijh/dot_general | solution.py:26
  22.3 2.6 %collective-permute-start.5 = (bf16[32,16,128]{2,1,0:T(8,128)(2,1)S(1)}, bf16[32,16,128]{2,1,0:T(8,128)(2,1)S(1)}, u32[]{:S(2)}, u32[]{:S(2)}) collective-permute-start(bf16[32,16,128]{2,1,0:T(8,128)(2,1)S(1)} %collective-permute-done.4), channel_id=1, source_target_pairs={{1,0},{2,1},{3,2},{4,3},{5,4},{6,5},{7,6},{0,7},{9,8},{10,9},{11,1... | collective-permute-start | bytes 393224 | tf_op jit(solution)/shard_map/ppermute | solution.py:58
  24.9 3.6 %collective-permute-done.2 = bf16[32,16,128]{2,1,0:T(8,128)(2,1)S(1)} collective-permute-done((bf16[32,16,128]{2,1,0:T(8,128)(2,1)S(1)}, bf16[32,16,128]{2,1,0:T(8,128)(2,1)S(1)}, u32[]{:S(2)}, u32[]{:S(2)}) %collective-permute-start.2) | collective-permute-done | bytes 131104 | tf_op jit(solution)/shard_map/ppermute | solution.py:53
  28.6 2.7 %collective-permute-start.6 = (bf16[32,16,128]{2,1,0:T(8,128)(2,1)S(1)}, bf16[32,16,128]{2,1,0:T(8,128)(2,1)S(1)}, u32[]{:S(2)}, u32[]{:S(2)}) collective-permute-start(bf16[32,16,128]{2,1,0:T(8,128)(2,1)S(1)} %collective-permute-done.5), channel_id=1, source_target_pairs={{1,0},{2,1},{3,2},{4,3},{5,4},{6,5},{7,6},{0,7},{9,8},{10,9},{11,1... | collective-permute-start | bytes 393224 | tf_op jit(solution)/shard_map/ppermute | solution.py:58
  31.3 3.7 %collective-permute-done.3 = bf16[32,16,128]{2,1,0:T(8,128)(2,1)S(1)} collective-permute-done((bf16[32,16,128]{2,1,0:T(8,128)(2,1)S(1)}, bf16[32,16,128]{2,1,0:T(8,128)(2,1)S(1)}, u32[]{:S(2)}, u32[]{:S(2)}) %collective-permute-start.3) | collective-permute-done | bytes 131104 | tf_op jit(solution)/shard_map/ppermute | solution.py:53
  35.1 4.1 %all-gather.2.cloned.1.call-done = bf16[32,128,128]{2,1,0:T(8,128)(2,1)} async-done(((bf16[32,16,128]{2,1,0:T(8,128)(2,1)}), bf16[32,128,128]{2,1,0:T(8,128)(2,1)}) %all-gather.2.cloned.1.call-update) | async-done | bytes 1048592 | tf_op jit(solution)/shard_map/all_gather | solution.py:40
  39.1 1.9 %dynamic-slice_select_fusion = bf16[16,128,128]{2,1,0:T(8,128)(2,1)} fusion(bf16[32,128,128]{2,1,0:T(8,128)(2,1)} %all-gather.2.cloned.1.call-done, s32[]{:T(128)S(6)} %select_n.48, pred[]{:T(512)S(6)} %eq.7), kind=kLoop, calls=%fused_computation.22 | loop fusion | flops 262144 | bytes 1048581 | tf_op jit(solution)/shard_map/jit(_where)/select_n | solution.py:14
  41.2 0.7 gather_fusion
  41.9 0.3 copy.38
  42.2 1.0 %copy.40 = bf16[32,128,128]{1,0,2:T(8,128)(2,1)S(1)} copy(bf16[32,128,128]{2,1,0:T(8,128)(2,1)S(1)} %bitcast.44) | data formatting | bytes 2097152 | tf_op jit(solution)/shard_map/reshape | solution.py:10
  43.2 37.6 %all-reduce.2.cloned.1.call-done = bf16[16,128,128]{2,1,0:T(8,128)(2,1)} async-done(((bf16[16,128,128]{2,1,0:T(8,128)(2,1)}), bf16[16,128,128]{2,1,0:T(8,128)(2,1)}) %all-reduce.2.cloned.1.call-update) | async-done | bytes 524304 | tf_op jit(solution)/shard_map/psum | solution.py:15
  80.8 1.5 %copy.39 = bf16[16,128,128]{1,0,2:T(8,128)(2,1)S(1)} copy(bf16[16,128,128]{2,1,0:T(8,128)(2,1)} %all-reduce.2.cloned.1.call-done) | data formatting | bytes 1048576 | tf_op jit(solution)/shard_map/psum | solution.py:15
  82.3 0.7 fusion.30
  82.9 0.2 multiply_reduce_fusion
  83.2 0.6 copy-done.7
  83.8 0.2 multiply_convert_fusion
  84.0 0.5 copy.41
  84.5 0.4 copy-done.2
  85.0 0.8 fusion.11
  (43 shorter events, 0.5 us)
Async XLA Ops:
  6.5 1.7 %copy-start = (bf16[128,128]{1,0:T(8,128)(2,1)S(1)}, bf16[128,128]{1,0:T(8,128)(2,1)}, u32[]{:S(2)}) copy-start(bf16[128,128]{1,0:T(8,128)(2,1)} %param.11) | copy-start | bytes 98308
  6.5 1.3 %copy-start.1 = (bf16[32,16,128]{2,1,0:T(8,128)(2,1)S(1)}, bf16[32,16,128]{2,1,0:T(8,128)(2,1)}, u32[]{:S(2)}) copy-start(bf16[32,16,128]{2,1,0:T(8,128)(2,1)} %param.9) | copy-start | bytes 393220
  6.5 32.6 %all-gather.2.cloned.1.call-start = ((), (), s32[]{:S(2)}) async-start(), calls=%async_computation | async-start | bytes 1179648 | tf_op jit(solution)/shard_map/all_gather | solution.py:40
  8.1 0.7 copy-start.6
  8.8 0.8 copy-start.4
  9.6 0.9 copy-start.8
  9.9 0.9 copy-start.5
  9.9 6.1 %collective-permute-start = (bf16[32,16,128]{2,1,0:T(8,128)(2,1)S(1)}, bf16[32,16,128]{2,1,0:T(8,128)(2,1)S(1)}, u32[]{:S(2)}, u32[]{:S(2)}) collective-permute-start(bf16[32,16,128]{2,1,0:T(8,128)(2,1)S(1)} %fusion.10), channel_id=1, source_target_pairs={{0,1},{1,2},{2,3},{3,4},{4,5},{5,6},{6,7},{7,0},{8,9},{9,10},{10,1... | collective-permute-start | bytes 393224 | tf_op jit(solution)/shard_map/ppermute | solution.py:53
  11.8 9.5 %copy-start.9 = (bf16[128,128]{1,0:T(8,128)(2,1)S(1)}, bf16[128,128]{1,0:T(8,128)(2,1)}, u32[]{:S(2)}) copy-start(bf16[128,128]{1,0:T(8,128)(2,1)} %param.16) | copy-start | bytes 98308
  11.8 69.0 %all-reduce.2.cloned.1.call-start = ((), (), s32[]{:S(2)}) async-start(), calls=%async_computation.1 | async-start | bytes 1048576 | tf_op jit(solution)/shard_map/psum | solution.py:15
  16.0 5.3 %collective-permute-start.1 = (bf16[32,16,128]{2,1,0:T(8,128)(2,1)S(1)}, bf16[32,16,128]{2,1,0:T(8,128)(2,1)S(1)}, u32[]{:S(2)}, u32[]{:S(2)}) collective-permute-start(bf16[32,16,128]{2,1,0:T(8,128)(2,1)S(1)} %collective-permute-done), channel_id=1, source_target_pairs={{0,1},{1,2},{2,3},{3,4},{4,5},{5,6},{6,7},{7,0},{8,9},{9,10},{10,1... | collective-permute-start | bytes 393224 | tf_op jit(solution)/shard_map/ppermute | solution.py:53
  16.0 6.3 %collective-permute-start.4 = (bf16[32,16,128]{2,1,0:T(8,128)(2,1)S(1)}, bf16[32,16,128]{2,1,0:T(8,128)(2,1)S(1)}, u32[]{:S(2)}, u32[]{:S(2)}) collective-permute-start(bf16[32,16,128]{2,1,0:T(8,128)(2,1)S(1)} %fusion.10), channel_id=1, source_target_pairs={{1,0},{2,1},{3,2},{4,3},{5,4},{6,5},{7,6},{0,7},{9,8},{10,9},{11,1... | collective-permute-start | bytes 393224 | tf_op jit(solution)/shard_map/ppermute | solution.py:58
  21.3 7.3 %collective-permute-start.2 = (bf16[32,16,128]{2,1,0:T(8,128)(2,1)S(1)}, bf16[32,16,128]{2,1,0:T(8,128)(2,1)S(1)}, u32[]{:S(2)}, u32[]{:S(2)}) collective-permute-start(bf16[32,16,128]{2,1,0:T(8,128)(2,1)S(1)} %collective-permute-done.1), channel_id=1, source_target_pairs={{0,1},{1,2},{2,3},{3,4},{4,5},{5,6},{6,7},{7,0},{8,9},{9,10},{10,1... | collective-permute-start | bytes 393224 | tf_op jit(solution)/shard_map/ppermute | solution.py:53
  22.3 6.3 %collective-permute-start.5 = (bf16[32,16,128]{2,1,0:T(8,128)(2,1)S(1)}, bf16[32,16,128]{2,1,0:T(8,128)(2,1)S(1)}, u32[]{:S(2)}, u32[]{:S(2)}) collective-permute-start(bf16[32,16,128]{2,1,0:T(8,128)(2,1)S(1)} %collective-permute-done.4), channel_id=1, source_target_pairs={{1,0},{2,1},{3,2},{4,3},{5,4},{6,5},{7,6},{0,7},{9,8},{10,9},{11,1... | collective-permute-start | bytes 393224 | tf_op jit(solution)/shard_map/ppermute | solution.py:58
  28.5 6.5 %collective-permute-start.3 = (bf16[32,16,128]{2,1,0:T(8,128)(2,1)S(1)}, bf16[32,16,128]{2,1,0:T(8,128)(2,1)S(1)}, u32[]{:S(2)}, u32[]{:S(2)}) collective-permute-start(bf16[32,16,128]{2,1,0:T(8,128)(2,1)S(1)} %collective-permute-done.2), channel_id=1, source_target_pairs={{0,1},{1,2},{2,3},{3,4},{4,5},{5,6},{6,7},{7,0},{8,9},{9,10},{10,1... | collective-permute-start | bytes 393224 | tf_op jit(solution)/shard_map/ppermute | solution.py:53
  28.6 12.5 %collective-permute-start.6 = (bf16[32,16,128]{2,1,0:T(8,128)(2,1)S(1)}, bf16[32,16,128]{2,1,0:T(8,128)(2,1)S(1)}, u32[]{:S(2)}, u32[]{:S(2)}) collective-permute-start(bf16[32,16,128]{2,1,0:T(8,128)(2,1)S(1)} %collective-permute-done.5), channel_id=1, source_target_pairs={{1,0},{2,1},{3,2},{4,3},{5,4},{6,5},{7,6},{0,7},{9,8},{10,9},{11,1... | collective-permute-start | bytes 393224 | tf_op jit(solution)/shard_map/ppermute | solution.py:58
  83.1 0.7 copy-start.7
  84.0 1.0 %copy-start.2 = (f32[32,16,128]{2,1,0:T(8,128)S(1)}, f32[32,16,128]{2,1,0:T(8,128)}, u32[]{:S(2)}) copy-start(f32[32,16,128]{2,1,0:T(8,128)} %fusion.8) | copy-start | bytes 786436
  84.0 0.9 %copy-start.3 = (bf16[128,128]{1,0:T(8,128)(2,1)S(1)}, bf16[128,128]{1,0:T(8,128)(2,1)}, u32[]{:S(2)}) copy-start(bf16[128,128]{1,0:T(8,128)(2,1)} %param.17) | copy-start | bytes 98308
Sparse Core Ops, SparseCore 0:
  11.9 27.1 all-gather.1
  41.5 39.2 all-reduce.1
